TPU v7x, 256 devices: a whole 4x4x8 slice. The times are simulated.
256 devices in a mesh: leaf: 32 (over x, z), row: 8 (over y, core).
Axes of the slice: x: 4, y: 4, z: 8, core: 2. Of those that a mesh axis runs over, the one named last changes fastest.
Arguments:
- leaf_probes: bfloat16 [32, 2048, 128], P('leaf', 'row'), may hold values from -6 to 6
- lower_probes: bfloat16 [4, 4096, 128], P(None, ('leaf', 'row')), may hold values from -6 to 6
- middle_probes: bfloat16 [2, 8192, 128], P(None, ('leaf', 'row')), may hold values from -6 to 6
- root_probes: bfloat16 [16384, 128], P(('leaf', 'row')), may hold values from -6 to 6
- leaf_inverse: bfloat16 [32, 2048, 2048], P('leaf', 'row'), as said below
- lower_inverse: bfloat16 [4, 4096, 4096], P(None, 'row', 'leaf'), as said below
- middle_inverse: bfloat16 [2, 8192, 8192], P(None, 'row', 'leaf'), as said below
- root_inverse: bfloat16 [16384, 16384], P('row', 'leaf'), as said below
- leaf_panel: bfloat16 [32, 512, 2048], P('leaf', 'row'), may hold values from -0.09375 to 0.09375
- lower_to_middle: bfloat16 [4, 8192, 4096], P(None, 'leaf', 'row'), may hold values from -0.125 to 0.125
- lower_to_root: bfloat16 [4, 16384, 4096], P(None, 'leaf', 'row'), may hold values from -0.125 to 0.125
- middle_to_root: bfloat16 [2, 16384, 8192], P(None, 'leaf', 'row'), may hold values from -0.09375 to 0.09375
- leaf_parent: int32 [32], replicated, may hold values from 0 to 3
- leaf_blocks: int32 [32, 4], replicated, may hold values from 0 to 127, as said below
Outputs:
- leaf_solution: bfloat16 [32, 2048, 128], P('leaf', 'row')
- lower_solution: bfloat16 [4, 4096, 128], P(None, ('leaf', 'row'))
- middle_solution: bfloat16 [2, 8192, 128], P(None, ('leaf', 'row'))
- root_solution: bfloat16 [16384, 128], P(('leaf', 'row'))
Inputs may be any that keep to these rules, and one draw needn't show every extreme that they name: `leaf_inverse`: every inverse of a diagonal factor block is lower triangular: entries above its diagonal are zero. `lower_inverse`: every inverse of a diagonal factor block is lower triangular: entries above its diagonal are zero. `middle_inverse`: every inverse of a diagonal factor block is lower triangular: entries above its diagonal are zero. `root_inverse`: every inverse of a diagonal factor block is lower triangular: entries above its diagonal are zero. `leaf_blocks`: columns 0 and 1 are two different blocks of 128 rows of the parent separator, column 2 a block of the second-level separator above it, column 3 a block of the root.
All inputs are finite; a program needn't handle non-finite values.
Results may differ from a plain program's by a relative error of at most 0.04.
Values may be sent and summed in bfloat16 or wider, within the bound.
No kernel may reach another device: no remote copies, remote signals or barrier semaphores. Data moves between devices by JAX's collectives and lax.ppermute only.
A program may use at most 64 MiB of HBM per device.

v0:
```python
import jax
import jax.numpy as jnp
from jax import lax
from jax.sharding import PartitionSpec as P

LOWER_ORDER = 4096
MIDDLE_ORDER = 8192
ROOT_ORDER = 16384
BLOCK = 128
PANEL = 512


def row_gather(pieces):
    return lax.all_gather(pieces, "row", axis=1, tiled=True)


def row_total(summands):
    return lax.psum_scatter(
        summands.astype(jnp.bfloat16), "row", scatter_dimension=1, tiled=True
    ).astype(jnp.float32)


def leaf_gather(pieces):
    return lax.all_gather(pieces, "leaf", axis=1, tiled=True)


def leaf_total(summands):
    return lax.psum_scatter(
        summands.astype(jnp.bfloat16), "leaf", scatter_dimension=1, tiled=True
    ).astype(jnp.float32)


def panel_targets(leaf_parent, leaf_blocks, length):
    row_ids = jnp.arange(length, dtype=jnp.int32)
    block_index = (row_ids // BLOCK)[None, :]
    offset = (row_ids % BLOCK)[None, :]
    chosen = jnp.where(
        block_index == 0,
        leaf_blocks[:, 0:1],
        jnp.where(
            block_index == 1,
            leaf_blocks[:, 1:2],
            jnp.where(block_index == 2, leaf_blocks[:, 2:3], leaf_blocks[:, 3:4]),
        ),
    )
    parent = leaf_parent[:, None]
    levels = jnp.where(block_index < 2, 2, jnp.where(block_index == 2, 1, 0)) + 0 * parent
    owners = jnp.where(block_index < 2, parent, jnp.where(block_index == 2, parent // 2, 0))
    return (levels, owners, chosen * BLOCK + offset)


def selector(targets, level_code, separators, window_start, window):
    levels, owners, places = targets
    inside = (levels == level_code) & (places >= window_start) & (places < window_start + window)
    flat_slot = jnp.where(inside, owners * window + places - window_start, -1).reshape(-1)
    slot_ids = jnp.arange(separators * window, dtype=jnp.int32)
    return (slot_ids[:, None] == flat_slot[None, :]).astype(jnp.bfloat16)


def level_forward(inverse, columns):
    summed_part = jnp.einsum("smn,snp->smp", inverse, columns, preferred_element_type=jnp.float32)
    return leaf_total(summed_part).astype(jnp.bfloat16)


def level_backward(inverse, row_block):
    summed_part = jnp.einsum("smn,smp->snp", inverse, row_block, preferred_element_type=jnp.float32)
    return row_total(summed_part).astype(jnp.bfloat16)


def body(
    leaf_probes,
    lower_probes,
    middle_probes,
    root_probes,
    leaf_inverse,
    lower_inverse,
    middle_inverse,
    root_inverse,
    leaf_panel,
    lower_to_middle,
    lower_to_root,
    middle_to_root,
    leaf_parent,
    leaf_blocks,
):
    leaf_devices = lax.axis_size("leaf")
    row_devices = lax.axis_size("row")
    leaf_index = lax.axis_index("leaf")
    row_index = lax.axis_index("row")
    position = leaf_index * row_devices + row_index
    probe_count = leaf_probes.shape[-1]
    root_pieces = root_probes[None]
    root_tiles = root_inverse[None]
    orders = (LOWER_ORDER, MIDDLE_ORDER, ROOT_ORDER)
    counts = (4, 2, 1)
    level_codes = (2, 1, 0)
    leaf_columns = row_gather(leaf_probes)
    leaf_solved = jnp.einsum(
        "lab,lbp->lap", leaf_inverse, leaf_columns, preferred_element_type=jnp.float32
    ).astype(jnp.bfloat16)
    leaf_whole = row_gather(leaf_solved)
    leaf_update = jnp.einsum(
        "lkb,lbp->lkp", leaf_panel, leaf_whole, preferred_element_type=jnp.float32
    ).astype(jnp.bfloat16)
    received = leaf_gather(row_gather(leaf_update))[0]
    targets = panel_targets(leaf_parent, leaf_blocks, PANEL)
    windows = [level_order // (leaf_devices * row_devices) for level_order in orders]
    pickers = [
        selector(
            targets,
            level_codes[member],
            counts[member],
            position * windows[member],
            windows[member],
        )
        for member in range(3)
    ]
    added = [
        jnp.dot(pickers[member], received, preferred_element_type=jnp.float32).reshape(
            counts[member], windows[member], probe_count
        )
        for member in range(3)
    ]
    lower_input = (lower_probes.astype(jnp.float32) - added[0]).astype(jnp.bfloat16)
    lower_solved = level_forward(lower_inverse, row_gather(lower_input))
    lower_block = leaf_gather(lower_solved)
    to_middle = jnp.einsum(
        "san,snp->sap", lower_to_middle, lower_block, preferred_element_type=jnp.float32
    )
    to_middle = to_middle.reshape(2, 2, to_middle.shape[1], probe_count).sum(axis=1)
    to_root = jnp.einsum(
        "san,snp->sap", lower_to_root, lower_block, preferred_element_type=jnp.float32
    ).sum(axis=0, keepdims=True)
    middle_total = row_total(to_middle) + added[1]
    middle_input = (middle_probes.astype(jnp.float32) - middle_total).astype(jnp.bfloat16)
    root_early = row_total(to_root)
    middle_solved = level_forward(middle_inverse, row_gather(middle_input))
    middle_block = leaf_gather(middle_solved)
    from_middle = jnp.einsum(
        "san,snp->sap", middle_to_root, middle_block, preferred_element_type=jnp.float32
    ).sum(axis=0, keepdims=True)
    root_total = root_early + row_total(from_middle)
    root_total = root_total + added[2]
    root_input = (root_pieces.astype(jnp.float32) - root_total).astype(jnp.bfloat16)
    root_solved = level_forward(root_tiles, row_gather(root_input))
    root_solution = level_backward(root_tiles, leaf_gather(root_solved))
    root_columns = row_gather(root_solution)
    middle_drop = jnp.einsum(
        "san,ap->snp", middle_to_root, root_columns[0], preferred_element_type=jnp.float32
    )
    middle_reduced = (middle_solved.astype(jnp.float32) - leaf_total(middle_drop)).astype(
        jnp.bfloat16
    )
    middle_solution = level_backward(middle_inverse, leaf_gather(middle_reduced))
    middle_columns = row_gather(middle_solution)
    parent_columns = jnp.repeat(middle_columns, 2, axis=0)
    lower_drop = jnp.einsum(
        "san,sap->snp", lower_to_middle, parent_columns, preferred_element_type=jnp.float32
    )
    lower_drop = lower_drop + jnp.einsum(
        "san,ap->snp", lower_to_root, root_columns[0], preferred_element_type=jnp.float32
    )
    lower_reduced = (lower_solved.astype(jnp.float32) - leaf_total(lower_drop)).astype(jnp.bfloat16)
    lower_solution = level_backward(lower_inverse, leaf_gather(lower_reduced))
    sources = (lower_solution, middle_solution, root_solution)
    values = sum(
        [
            jnp.einsum(
                "sm,sp->mp",
                pickers[member],
                sources[member].reshape(-1, probe_count),
                preferred_element_type=jnp.float32,
            )
            for member in range(3)
        ]
    )
    ancestor = row_total(leaf_total(values[None]))
    ancestor = ancestor.astype(jnp.bfloat16)
    leaf_back = row_total(
        jnp.einsum("lkb,lkp->lbp", leaf_panel, ancestor, preferred_element_type=jnp.float32)
    )
    leaf_reduced = (leaf_solved.astype(jnp.float32) - leaf_back).astype(jnp.bfloat16)
    leaf_solution = row_total(
        jnp.einsum("lab,lap->lbp", leaf_inverse, leaf_reduced, preferred_element_type=jnp.float32)
    ).astype(jnp.bfloat16)
    return (leaf_solution, lower_solution, middle_solution, root_solution[0])


def solution(mesh):
    placed = (
        P("leaf", "row", None),
        P(None, ("leaf", "row"), None),
        P(None, ("leaf", "row"), None),
        P(("leaf", "row"), None),
        P("leaf", "row", None),
        P(None, "row", "leaf"),
        P(None, "row", "leaf"),
        P("row", "leaf"),
        P("leaf", "row", None),
        P(None, "leaf", "row"),
        P(None, "leaf", "row"),
        P(None, "leaf", "row"),
        P(),
        P(),
    )
    return jax.shard_map(
        body,
        mesh=mesh,
        in_specs=placed,
        out_specs=(
            P("leaf", "row", None),
            P(None, ("leaf", "row"), None),
            P(None, ("leaf", "row"), None),
            P(("leaf", "row"), None),
        ),
        check_vma=False,
    )
```

profile of v0, /device:TPU:32, one launch (start us, length us, event | category | flops | bytes accessed | tf_op | source)
XLA Modules:
  0.0 1845.7 jit_solution(16149215589096796807)
XLA Ops:
  7.2 14.0 all_gather.42
  22.9 13.2 all-gather
  37.3 13.8 all-gather.1
  54.3 80.9 %all-gather.5.cloned.1.call-done = bf16[16384,128]{1,0:T(8,128)(2,1)} async-done(((bf16[512,128]{1,0:T(8,128)(2,1)}), bf16[16384,128]{1,0:T(8,128)(2,1)}) %all-gather.5.cloned.1.call-update) | async-done | bytes 4194320 | tf_op jit(solution)/shard_map/all_gather | solution.py:24
  154.2 141.7 %all-reduce.13.cloned.1.call-done = bf16[4,512,128]{2,0,1:T(4,128)(2,1)} async-done(((bf16[4,512,128]{2,0,1:T(4,128)(2,1)}), bf16[4,512,128]{2,0,1:T(4,128)(2,1)}) %all-reduce.13.cloned.1.call-update) | async-done | bytes 524304
  296.7 47.8 %all_gather.47 = bf16[4,512,128]{2,0,1:T(4,128)(2,1)S(1)} all-gather(bf16[4,16,128]{2,0,1:T(4,128)(2,1)S(1)} %constant_dynamic-slice_fusion.3), channel_id=1, replica_groups=mesh['leaf'=32,'row'=8] {'leaf'}, dimensions={1}, use_global_device_ids=true | all-gather | bytes 540672 | tf_op jit(solution)/shard_map/all_gather | solution.py:24
  348.0 31.0 %reduce-scatter.18.cloned.1.call-done = bf16[2,32,128]{2,1,0:T(8,128)(2,1)} async-done(((bf16[2,256,128]{2,1,0:T(8,128)(2,1)}), bf16[2,32,128]{2,1,0:T(8,128)(2,1)}) %reduce-scatter.18.cloned.1.call-update) | async-done | bytes 16400 | tf_op jit(solution)/shard_map/reduce_scatter | solution.py:18
  400.6 142.2 %all-reduce.15.cloned.1.call-done = bf16[2,1024,128]{2,0,1:T(2,128)(2,1)} async-done(((bf16[2,1024,128]{2,0,1:T(2,128)(2,1)}), bf16[2,1024,128]{2,0,1:T(2,128)(2,1)}) %all-reduce.15.cloned.1.call-update) | async-done | bytes 524304
  543.5 47.8 %all_gather.49 = bf16[2,1024,128]{2,0,1:T(2,128)(2,1)S(1)} all-gather(bf16[2,32,128]{2,0,1:T(2,128)(2,1)S(1)} %constant_dynamic-slice_fusion.2), channel_id=1, replica_groups=mesh['leaf'=32,'row'=8] {'leaf'}, dimensions={1}, use_global_device_ids=true | all-gather | bytes 540672 | tf_op jit(solution)/shard_map/all_gather | solution.py:24
  595.5 31.1 %reduce-scatter.30.cloned.1.call-done = bf16[64,128]{1,0:T(8,128)(2,1)} async-done(((bf16[512,128]{1,0:T(8,128)(2,1)}), bf16[64,128]{1,0:T(8,128)(2,1)}) %reduce-scatter.30.cloned.1.call-update) | async-done | bytes 16400
  648.2 212.2 %reduce-scatter.32.cloned.1.call-done = bf16[64,128]{1,0:T(8,128)(2,1)} async-done(((bf16[2048,128]{1,0:T(8,128)(2,1)}), bf16[64,128]{1,0:T(8,128)(2,1)}) %reduce-scatter.32.cloned.1.call-update) | async-done | bytes 16400
  861.2 48.2 %all_gather.51 = bf16[1,2048,128]{2,1,0:T(8,128)(2,1)S(1)} all-gather(bf16[1,64,128]{2,1,0:T(8,128)(2,1)S(1)} %copy.54), channel_id=1, replica_groups=mesh['leaf'=32,'row'=8] {'leaf'}, dimensions={1}, use_global_device_ids=true | all-gather | bytes 540672 | tf_op jit(solution)/shard_map/all_gather | solution.py:24
  910.8 32.2 %reduce-scatter.34.cloned.1.call-done = bf16[64,128]{1,0:T(8,128)(2,1)} async-done(((bf16[512,128]{1,0:T(8,128)(2,1)}), bf16[64,128]{1,0:T(8,128)(2,1)}) %reduce-scatter.34.cloned.1.call-update) | async-done | bytes 16400
  962.1 146.2 %all-reduce.17.cloned.1.call-done = bf16[2,1024,128]{2,0,1:T(2,128)(2,1)} async-done(((bf16[2,1024,128]{2,0,1:T(2,128)(2,1)}), bf16[2,1024,128]{2,0,1:T(2,128)(2,1)}) %all-reduce.17.cloned.1.call-update) | async-done | bytes 524304
  1109.0 47.8 %all_gather.53 = bf16[2,1024,128]{2,0,1:T(2,128)(2,1)S(1)} all-gather(bf16[2,32,128]{2,0,1:T(2,128)(2,1)S(1)} %subtract_convert_fusion.1), channel_id=1, replica_groups=mesh['leaf'=32,'row'=8] {'leaf'}, dimensions={1}, use_global_device_ids=true | all-gather | bytes 540672 | tf_op jit(solution)/shard_map/all_gather | solution.py:24
  1162.1 62.1 %all-reduce.19.cloned.1.call-done = bf16[2,256,128]{2,0,1:T(2,128)(2,1)} async-done(((bf16[2,256,128]{2,0,1:T(2,128)(2,1)}), bf16[2,256,128]{2,0,1:T(2,128)(2,1)}) %all-reduce.19.cloned.1.call-update) | async-done | bytes 131088
  1224.9 13.8 all_gather.54
  1244.9 146.3 %all-reduce.21.cloned.1.call-done = bf16[4,512,128]{2,0,1:T(4,128)(2,1)} async-done(((bf16[4,512,128]{2,0,1:T(4,128)(2,1)}), bf16[4,512,128]{2,0,1:T(4,128)(2,1)}) %all-reduce.21.cloned.1.call-update) | async-done | bytes 524304
  1391.9 47.8 %all_gather.55 = bf16[4,512,128]{2,0,1:T(4,128)(2,1)S(1)} all-gather(bf16[4,16,128]{2,0,1:T(4,128)(2,1)S(1)} %subtract_convert_fusion), channel_id=1, replica_groups=mesh['leaf'=32,'row'=8] {'leaf'}, dimensions={1}, use_global_device_ids=true | all-gather | bytes 540672 | tf_op jit(solution)/shard_map/all_gather | solution.py:24
  1443.0 62.3 %all-reduce.23.cloned.1.call-done = bf16[4,128,128]{2,0,1:T(4,128)(2,1)} async-done(((bf16[4,128,128]{2,0,1:T(4,128)(2,1)}), bf16[4,128,128]{2,0,1:T(4,128)(2,1)}) %all-reduce.23.cloned.1.call-update) | async-done | bytes 131088
  1514.2 219.5 %reduce-scatter.20.cloned.1.call-done = bf16[1,512,128]{2,1,0:T(8,128)(2,1)} async-done(((bf16[1,16384,128]{2,1,0:T(8,128)(2,1)}), bf16[1,512,128]{2,1,0:T(8,128)(2,1)}) %reduce-scatter.20.cloned.1.call-update) | async-done | bytes 131088 | tf_op jit(solution)/shard_map/reduce_scatter | solution.py:28
  1733.7 34.3 %reduce-scatter.22.cloned.1.call-done = bf16[1,64,128]{2,1,0:T(8,128)(2,1)} async-done(((bf16[1,512,128]{2,1,0:T(8,128)(2,1)}), bf16[1,64,128]{2,1,0:T(8,128)(2,1)}) %reduce-scatter.22.cloned.1.call-update) | async-done | bytes 16400 | tf_op jit(solution)/shard_map/reduce_scatter | solution.py:18
  1770.0 32.9 %reduce-scatter.24.cloned.1.call-done = bf16[1,256,128]{2,1,0:T(8,128)(2,1)} async-done(((bf16[1,2048,128]{2,1,0:T(8,128)(2,1)}), bf16[1,256,128]{2,1,0:T(8,128)(2,1)}) %reduce-scatter.24.cloned.1.call-update) | async-done | bytes 65552 | tf_op jit(solution)/shard_map/reduce_scatter | solution.py:18
  1805.5 32.0 %reduce-scatter.26.cloned.1.call-done = bf16[1,256,128]{1,2,0:T(8,128)(2,1)} async-done(((bf16[1,2048,128]{1,2,0:T(8,128)(2,1)}), bf16[1,256,128]{1,2,0:T(8,128)(2,1)}) %reduce-scatter.26.cloned.1.call-update) | async-done | bytes 65552 | tf_op jit(solution)/shard_map/reduce_scatter | solution.py:18
  (153 shorter events, 127.3 us)
Async XLA Ops:
  7.2 636.1 %copy-start = (bf16[2048,512]{1,0:T(8,128)(2,1)S(1)}, bf16[2048,512]{1,0:T(8,128)(2,1)}, u32[]{:S(2)}) copy-start(bf16[2048,512]{1,0:T(8,128)(2,1)} %param.21) | copy-start | bytes 6291460
  7.2 128.0 %all-gather.5.cloned.1.call-start = ((), (), s32[]{:S(2)}) async-start(), calls=%async_computation.14 | async-start | bytes 4325376 | tf_op jit(solution)/shard_map/all_gather | solution.py:24
  51.2 244.8 %all-reduce.13.cloned.1.call-start = ((), (), s32[]{:S(2)}) async-start(), calls=%async_computation.19 | async-start | bytes 1048576
  152.9 226.0 %reduce-scatter.18.cloned.1.call-start = ((), (), s32[]{:S(2)}) async-start(), calls=%async_computation.9 | async-start | bytes 147456 | tf_op jit(solution)/shard_map/reduce_scatter | solution.py:18
  347.0 195.8 %all-reduce.15.cloned.1.call-start = ((), (), s32[]{:S(2)}) async-start(), calls=%async_computation.20 | async-start | bytes 1048576
  396.5 230.8 %copy-start.13 = (bf16[64,128]{1,0:T(8,128)(2,1)S(1)}, bf16[64,128]{1,0:T(8,128)(2,1)}, u32[]{:S(2)}) copy-start(bf16[64,128]{1,0:T(8,128)(2,1)} %param.17) | copy-start | bytes 49156
  396.5 198.2 %reduce-scatter.28.cloned.1.call-start = ((), (), s32[]{:S(2)}) async-start(), calls=%async_computation.15 | async-start | bytes 147456
  400.5 226.1 %reduce-scatter.30.cloned.1.call-start = ((), (), s32[]{:S(2)}) async-start(), calls=%async_computation.16 | async-start | bytes 147456
  594.6 265.8 %reduce-scatter.32.cloned.1.call-start = ((), (), s32[]{:S(2)}) async-start(), calls=%async_computation.17 | async-start | bytes 540672
  648.2 294.9 %reduce-scatter.34.cloned.1.call-start = ((), (), s32[]{:S(2)}) async-start(), calls=%async_computation.18 | async-start | bytes 147456
  909.9 250.9 %copy-start.20 = (u32[256]{0:T(256)S(1)}, u32[256]{0:T(256)}, u32[]{:S(2)}) copy-start(u32[256]{0:T(256)} %constant.105) | copy-start | bytes 3076
  910.8 330.6 %copy-start.1 = (bf16[4,256,512]{2,1,0:T(8,128)(2,1)S(1)}, bf16[4,256,512]{2,1,0:T(8,128)(2,1)}, u32[]{:S(2)}) copy-start(bf16[4,256,512]{2,1,0:T(8,128)(2,1)} %param.23) | copy-start | bytes 3145732
  910.8 197.5 %all-reduce.17.cloned.1.call-start = ((), (), s32[]{:S(2)}) async-start(), calls=%async_computation.21 | async-start | bytes 1048576
  962.0 262.1 %all-reduce.19.cloned.1.call-start = ((), (), s32[]{:S(2)}) async-start(), calls=%async_computation.22 | async-start | bytes 262144
  1160.8 230.4 %all-reduce.21.cloned.1.call-start = ((), (), s32[]{:S(2)}) async-start(), calls=%async_computation.23 | async-start | bytes 1048576
  1241.6 201.2 %copy-start.7 = (bf16[1,64,128]{2,0,1:T(2,128)(2,1)S(1)}, bf16[1,64,128]{2,0,1:T(2,128)(2,1)}, u32[]{:S(2)}) copy-start(bf16[1,64,128]{2,0,1:T(2,128)(2,1)} %copy-done.6) | copy-start | bytes 49156
  1244.8 260.5 %all-reduce.23.cloned.1.call-start = ((), (), s32[]{:S(2)}) async-start(), calls=%async_computation.24 | async-start | bytes 262144
  1441.9 291.7 %reduce-scatter.20.cloned.1.call-start = ((), (), s32[]{:S(2)}) async-start(), calls=%async_computation.10 | async-start | bytes 4325376 | tf_op jit(solution)/shard_map/reduce_scatter | solution.py:28
  1514.1 253.9 %copy-start.5 = (bf16[1,64,2048]{2,1,0:T(8,128)(2,1)S(1)}, bf16[1,64,2048]{2,1,0:T(8,128)(2,1)}, u32[]{:S(2)}) copy-start(bf16[1,64,2048]{2,1,0:T(8,128)(2,1)} %param.22) | copy-start | bytes 786436
  1514.1 288.8 %copy-start.2 = (bf16[1,256,2048]{2,1,0:T(8,128)(2,1)S(1)}, bf16[1,256,2048]{2,1,0:T(8,128)(2,1)}, u32[]{:S(2)}) copy-start(bf16[1,256,2048]{2,1,0:T(8,128)(2,1)} %param.18) | copy-start | bytes 3145732
  1514.1 290.8 %copy-start.8 = (bf16[1,64,128]{2,0,1:T(2,128)(2,1)S(1)}, bf16[1,64,128]{2,0,1:T(2,128)(2,1)}, u32[]{:S(2)}) copy-start(bf16[1,64,128]{2,0,1:T(2,128)(2,1)} %copy-done.6) | copy-start | bytes 49156
  1514.1 253.9 %reduce-scatter.22.cloned.1.call-start = ((), (), s32[]{:S(2)}) async-start(), calls=%async_computation.11 | async-start | bytes 147456 | tf_op jit(solution)/shard_map/reduce_scatter | solution.py:18
  1733.7 69.2 %reduce-scatter.24.cloned.1.call-start = ((), (), s32[]{:S(2)}) async-start(), calls=%async_computation.12 | async-start | bytes 589824 | tf_op jit(solution)/shard_map/reduce_scatter | solution.py:18
  1769.9 67.6 %reduce-scatter.26.cloned.1.call-start = ((), (), s32[]{:S(2)}) async-start(), calls=%async_computation.13 | async-start | bytes 589824 | tf_op jit(solution)/shard_map/reduce_scatter | solution.py:18
  (14 other events, 1164.2 us)
Sparse Core Ops, SparseCore 0:
  51.3 83.8 all-gather.4
  153.0 142.9 all-reduce.12
  347.1 31.7 reduce-scatter.17
  396.6 146.0 all-reduce.14
  545.3 30.8 reduce-scatter.27
  594.8 31.7 reduce-scatter.29
  648.3 212.1 reduce-scatter.31
  910.9 32.0 reduce-scatter.33
  962.2 146.0 all-reduce.16
  1160.9 63.2 all-reduce.18
  1244.9 146.1 all-reduce.20
  1442.0 63.2 all-reduce.22
  1514.3 219.3 reduce-scatter.19
  1736.0 31.9 reduce-scatter.21
  1770.5 32.3 reduce-scatter.23
  1805.3 32.2 reduce-scatter.25
where the time goes:
time: 1850 us
  waiting for transfers between devices  1410 us (76%)
  blocking collectives  346 us (19%)
  matrix products  42.3 us (2%)
  local copies, waits for them, and re-layouts  27.8 us (2%)
    unnamed x26, waiting for transfers between devices  977 us
    all_gather x5, blocking collectives, leaf_gather(): return lax.all_gather(pieces, 'leaf', axis=1, tiled=True)  240 us
    reduce_scatter x1, waiting for transfers between devices, leaf_total(): lax.psum_scatter(summands.astype(jnp.bfloat16), 'leaf', scatter_dimension...  219 us
    reduce_scatter x4, waiting for transfers between devices, row_total(): lax.psum_scatter(summands.astype(jnp.bfloat16), 'row', scatter_dimension=...  130 us
    all_gather x8, blocking collectives, row_gather(): return lax.all_gather(pieces, 'row', axis=1, tiled=True)  106 us
    all_gather x1, waiting for transfers between devices, leaf_gather(): return lax.all_gather(pieces, 'leaf', axis=1, tiled=True)  80.9 us
  transfers between devices with their start and end apart: 16, of which 15 were waited for; matrix products, arithmetic and copies ran while one was open for 1% of the time, Pallas kernels for 0%

commit v1 on v0

v1 whole, which is shorter than its diff:
```python
import jax
import jax.numpy as jnp
from jax import lax
from jax.sharding import Mesh, PartitionSpec as P

LEAF = ("x", "z")
ROW = ("y", "core")
LEAVES = 32
ROWS = 8
HALF = 64
F32 = jnp.float32
BF16 = jnp.bfloat16


def swap(pieces, axes):
    return lax.all_to_all(pieces, axes, split_axis=0, concat_axis=0, tiled=True)


def leaf_scatter(partial):
    pieces = partial.astype(BF16).reshape(LEAVES, HALF, -1)
    return jnp.sum(swap(pieces, LEAF).astype(F32), axis=0)


def leaf_gather(piece):
    pieces = swap(jnp.broadcast_to(piece[None], (LEAVES,) + piece.shape), LEAF)
    return pieces.reshape((-1,) + piece.shape[1:])


def row_scatter(partial):
    pieces = partial.astype(BF16).reshape(ROWS, -1, partial.shape[-1])
    return jnp.sum(swap(pieces, ROW).astype(F32), axis=0)


def row_gather(piece):
    return lax.all_gather(piece, ROW, axis=0, tiled=False)


def core_swap(half):
    return lax.ppermute(half, "core", [(0, 1), (1, 0)])


def both_halves(half, core):
    other = core_swap(half)
    first = jnp.where(core == 0, half, other)
    second = jnp.where(core == 0, other, half)
    return jnp.stack([first, second])


def row_half_sum(partial, core):
    rounded = partial.astype(BF16)
    mine = jnp.where(core == 0, partial[0], partial[1])
    theirs = jnp.where(core == 0, rounded[1], rounded[0])
    pair = (mine + core_swap(theirs).astype(F32)).astype(BF16)
    gathered = swap(jnp.broadcast_to(pair[None], (4,) + pair.shape), "y")
    return jnp.sum(gathered.astype(F32), axis=0)


def dot(spec, left, right):
    return jnp.einsum(spec, left, right, preferred_element_type=F32)


def body(
    leaf_probes,
    lower_probes,
    middle_probes,
    root_probes,
    leaf_inverse,
    lower_inverse,
    middle_inverse,
    root_inverse,
    leaf_panel,
    lower_to_middle,
    lower_to_root,
    middle_to_root,
    leaf_parent,
    leaf_blocks,
):
    leaf = lax.axis_index("x") * 8 + lax.axis_index("z")
    y = lax.axis_index("y")
    core = lax.axis_index("core")
    row = y * 2 + core
    probes = leaf_probes.shape[-1]
    inverse = leaf_inverse[0]
    panel = leaf_panel[0]

    block = lax.dynamic_index_in_dim(leaf_blocks, y, axis=1, keepdims=False)
    parent = leaf_parent
    slot = jnp.where(
        y < 2,
        jnp.where(block == leaf, parent, -1),
        jnp.where(
            y == 2,
            jnp.where(block // 2 == leaf, (parent // 2) * 2 + block % 2, -1),
            jnp.where(block // 4 == leaf, block % 4, -1),
        ),
    )
    chosen = (slot[None, :] == jnp.arange(4, dtype=jnp.int32)[:, None]).astype(F32)

    own = jnp.concatenate(
        [
            leaf_probes[0],
            lower_probes.reshape(-1, probes),
            middle_probes.reshape(-1, probes),
            root_probes,
        ]
    )
    held = row_gather(own)
    leaf_columns = held[:, :256].reshape(-1, probes)
    lower_own = held[:, 256:320].reshape(8, 4, 16, probes).transpose(1, 0, 2, 3).reshape(4, 2, HALF, probes)
    middle_own = held[:, 320:384].reshape(8, 2, 32, probes).transpose(1, 0, 2, 3).reshape(2, 256, probes)
    root_own = held[:, 384:].reshape(2, 256, probes)

    leaf_solved = dot("ab,bp->ap", inverse, leaf_columns).astype(BF16)
    leaf_whole = row_gather(leaf_solved).reshape(-1, probes)
    leaf_update = dot("kb,bp->kp", panel, leaf_whole).astype(BF16)
    received = swap(jnp.broadcast_to(leaf_update[None], (LEAVES, HALF, probes)), LEAF).astype(F32)
    landed = jnp.sum(chosen[:, :, None, None] * received[None], axis=1).astype(BF16)
    by_level = swap(jnp.broadcast_to(landed[None], (4,) + landed.shape), "y")
    lower_added = by_level[0].astype(F32) + by_level[1].astype(F32)
    lower_half = lax.dynamic_index_in_dim(lower_own, core, axis=1, keepdims=False)
    lower_half = (lower_half.astype(F32) - lower_added).astype(BF16)
    lower_input = both_halves(lower_half, core).transpose(1, 0, 2, 3).reshape(4, 128, probes)
    upper_added = both_halves(by_level[2:], core)
    middle_added = upper_added[:, 0].reshape(2, 2, 2, HALF, probes).transpose(1, 2, 0, 3, 4).reshape(2, 256, probes)
    root_added = upper_added[:, 1].transpose(1, 0, 2, 3).reshape(2, 256, probes)
    middle_base = middle_own.astype(F32) - middle_added.astype(F32)
    root_base = root_own.astype(F32) - root_added.astype(F32)

    lower_solved = leaf_scatter(dot("smn,snp->smp", lower_inverse, lower_input)).astype(BF16)
    lower_block = leaf_gather(lower_solved).reshape(4, 512, probes)
    to_middle = dot("san,snp->sap", lower_to_middle, lower_block)
    to_middle = to_middle.reshape(2, 2, 256, probes).sum(axis=1)
    middle_sum = row_half_sum(to_middle, core)
    middle_half = (lax.dynamic_index_in_dim(middle_base, core, axis=0, keepdims=False) - middle_sum).astype(BF16)
    middle_input = both_halves(middle_half, core)
    to_root = dot("san,snp->sap", lower_to_root, lower_block).sum(axis=0)

    middle_solved = leaf_scatter(dot("smn,snp->smp", middle_inverse, middle_input)).astype(BF16)
    middle_block = leaf_gather(middle_solved).reshape(2, 1024, probes)
    to_root = to_root + dot("san,snp->sap", middle_to_root, middle_block).sum(axis=0)
    root_sum = row_half_sum(to_root.reshape(2, 256, probes), core)
    root_half = (lax.dynamic_index_in_dim(root_base, core, axis=0, keepdims=False) - root_sum).astype(BF16)
    root_input = both_halves(root_half, core).reshape(512, probes)

    root_solved = leaf_scatter(dot("mn,np->mp", root_inverse, root_input)).astype(BF16)
    root_rows = leaf_gather(root_solved)
    root_half = row_half_sum(dot("mn,mp->np", root_inverse, root_rows).reshape(2, 256, probes), core).astype(BF16)
    root_columns = both_halves(root_half, core).reshape(512, probes)

    middle_drop = leaf_scatter(dot("san,ap->snp", middle_to_root, root_columns))
    middle_reduced = (middle_solved.astype(F32) - middle_drop).astype(BF16)
    middle_rows = leaf_gather(middle_reduced).reshape(2, 1024, probes)
    middle_half = row_half_sum(dot("smn,smp->snp", middle_inverse, middle_rows), core).astype(BF16)
    middle_columns = both_halves(middle_half, core)

    lower_drop = dot("san,ap->snp", lower_to_root, root_columns)
    lower_drop = lower_drop + dot(
        "qsan,qap->qsnp", lower_to_middle.reshape(2, 2, 256, 512), middle_columns
    ).reshape(4, 512, probes)
    lower_reduced = (lower_solved.astype(F32) - leaf_scatter(lower_drop)).astype(BF16)
    lower_rows = leaf_gather(lower_reduced).reshape(4, 512, probes)
    lower_half = row_half_sum(dot("smn,smp->snp", lower_inverse, lower_rows).reshape(2, 256, probes), core)
    lower_columns = both_halves(lower_half.astype(BF16), core).reshape(4, 128, probes)

    stacked = jnp.where(
        y < 2,
        lower_columns.reshape(4, 2, HALF, probes),
        jnp.where(
            y == 2,
            middle_columns.reshape(4, 2, HALF, probes),
            root_columns.reshape(4, 2, HALF, probes),
        ),
    )
    table = lax.dynamic_index_in_dim(stacked, core, axis=1, keepdims=False)
    sent = jnp.sum(chosen[:, :, None, None] * table[:, None].astype(F32), axis=0).astype(BF16)
    ancestor = jnp.sum(swap(sent, LEAF).astype(F32), axis=0).astype(BF16)
    leaf_back = row_scatter(dot("kb,kp->bp", panel, ancestor))
    leaf_reduced = (leaf_solved.astype(F32) - leaf_back).astype(BF16)
    leaf_solution = row_scatter(dot("ab,ap->bp", inverse, leaf_reduced)).astype(BF16)

    lower_solution = lax.dynamic_slice_in_dim(lower_columns, row * 16, 16, axis=1)
    middle_solution = lax.dynamic_slice_in_dim(middle_columns, row * 32, 32, axis=1)
    root_solution = lax.dynamic_slice_in_dim(root_columns, row * 64, 64, axis=0)
    return (leaf_solution[None], lower_solution, middle_solution, root_solution)


def solution(mesh):
    fine = Mesh(mesh.devices.reshape(4, 8, 4, 2), ("x", "z", "y", "core"))
    every = LEAF + ROW
    return jax.shard_map(
        body,
        mesh=fine,
        in_specs=(
            P(LEAF, ROW, None),
            P(None, every, None),
            P(None, every, None),
            P(every, None),
            P(LEAF, ROW, None),
            P(None, ROW, LEAF),
            P(None, ROW, LEAF),
            P(ROW, LEAF),
            P(LEAF, ROW, None),
            P(None, LEAF, ROW),
            P(None, LEAF, ROW),
            P(None, LEAF, ROW),
            P(),
            P(),
        ),
        out_specs=(
            P(LEAF, ROW, None),
            P(None, every, None),
            P(None, every, None),
            P(every, None),
        ),
        check_vma=False,
    )
```

time: 1850 us -> 444 us (0.24)
  waiting for transfers between devices: 1410 us -> 73.8 us
  blocking collectives: 346 us -> 294 us
  starting transfers between devices: 0.88 us -> 31.6 us
  matrix products: 42.3 us -> 14.1 us
    unnamed x26 -> x0, waiting for transfers between devices: 977 us -> none
    reduce_scatter x5 -> x0, waiting for transfers between devices: 350 us -> none  [the longest x1 219 us: leaf_total(): lax.psum_scatter(summands.astype(jnp.bfloat16), 'leaf', scatter_dimension...]
    all_gather x13 -> x2, blocking collectives: 346 us -> 27.3 us  [row_gather(): return lax.all_gather(piece, ROW, axis=0, tiled=False)]
    all_to_all x0 -> x14, blocking collectives: none -> 266 us  [swap(): return lax.all_to_all(pieces, axes, split_axis=0, concat_axis=0, tiled=True)]
    all_gather x1 -> x0, waiting for transfers between devices: 80.9 us -> none  [leaf_gather(): return lax.all_gather(pieces, 'leaf', axis=1, tiled=True)]
    all_to_all x0 -> x6, waiting for transfers between devices: none -> 61.4 us  [swap(): return lax.all_to_all(pieces, axes, split_axis=0, concat_axis=0, tiled=True)]
    all_to_all x0 -> x6, starting transfers between devices: none -> 30.3 us  [swap(): return lax.all_to_all(pieces, axes, split_axis=0, concat_axis=0, tiled=True)]
    dot_general x22 -> x16, matrix products: 42.3 us -> 14.1 us  [dot(): return jnp.einsum(spec, left, right, preferred_element_type=F32)]
  transfers between devices with their start and end apart: 16 -> 18, of which waited for: 15 -> 16; matrix products, arithmetic and copies ran while one was open for 1% -> 2% of each run, Pallas kernels for 0% -> 0%
where the time goes in v1:
time: 444 us; the launch traced here: 442 us
  blocking collectives  294 us (66%)
  waiting for transfers between devices  73.8 us (17%)
  starting transfers between devices  31.6 us (7%)
  local copies, waits for them, and re-layouts  16.6 us (4%)
  matrix products  14.1 us (3%)
  other arithmetic  10.7 us (2%)
    all_to_all x14, blocking collectives, swap(): return lax.all_to_all(pieces, axes, split_axis=0, concat_axis=0, tiled=True)  266 us
    all_to_all x6, waiting for transfers between devices, swap(): return lax.all_to_all(pieces, axes, split_axis=0, concat_axis=0, tiled=True)  61.4 us
    all_to_all x6, starting transfers between devices, swap(): return lax.all_to_all(pieces, axes, split_axis=0, concat_axis=0, tiled=True)  30.3 us
    all_gather x2, blocking collectives, row_gather(): return lax.all_gather(piece, ROW, axis=0, tiled=False)  27.3 us
    dot_general x16, matrix products, dot(): return jnp.einsum(spec, left, right, preferred_element_type=F32)  14.1 us
    ppermute x12, waiting for transfers between devices, core_swap(): return lax.ppermute(half, 'core', [(0, 1), (1, 0)])  12.4 us
  transfers between devices with their start and end apart: 18, of which 16 were waited for; matrix products, arithmetic and copies ran while one was open for 2% of the time, Pallas kernels for 0%

profile of v1, /device:TPU:32, one launch (start us, length us, event | category | flops | bytes accessed | tf_op | source)
XLA Modules:
  0.0 441.9 jit_solution(4643874270304660430)
XLA Ops:
  1.7 14.2 %all-gather = bf16[3584,128]{1,0:T(8,128)(2,1)S(1)} all-gather(bf16[448,128]{1,0:T(8,128)(2,1)S(1)} %pad_maximum_fusion.5), channel_id=2, replica_groups=mesh['x'=4,'z'=8,'y'=4,'core'=2] {'y','core'}, dimensions={0}, use_global_device_ids=true | all-gather | bytes 1032192 | tf_op jit(solution)/shard_map/all_gather | solution.py:35
  16.5 13.1 %all-gather.1 = bf16[2048,128]{0,1:T(8,128)(2,1)S(1)} all-gather(bf16[256,128]{0,1:T(8,128)(2,1)S(1)} %fusion.8), channel_id=3, replica_groups=mesh['x'=4,'z'=8,'y'=4,'core'=2] {'y','core'}, dimensions={0}, use_global_device_ids=true | all-gather | bytes 589824 | tf_op jit(solution)/shard_map/all_gather | solution.py:35
  30.8 11.1 %all-to-all-start = ((bf16[32,64,128]{2,1,0:T(8,128)(2,1)}), bf16[32,64,128]{2,1,0:T(8,128)(2,1)S(1)}, u32[]{:S(2)}, u32[]{:S(2)}) async-start(bf16[32,64,128]{2,1,0:T(8,128)(2,1)} %broadcast_in_dim.33), calls=%async_computation | async-start | bytes 1048576 | tf_op jit(solution)/shard_map/all_to_all | solution.py:16
  42.7 17.4 %all-to-all-done = bf16[32,64,128]{2,1,0:T(8,128)(2,1)S(1)} async-done(((bf16[32,64,128]{2,1,0:T(8,128)(2,1)}), bf16[32,64,128]{2,1,0:T(8,128)(2,1)S(1)}, u32[]{:S(2)}, u32[]{:S(2)}) %all-to-all-start) | async-done | bytes 524320 | tf_op jit(solution)/shard_map/all_to_all | solution.py:16
  66.2 6.0 %all-to-all-done.1 = bf16[4,4,64,128]{3,2,1,0:T(8,128)(2,1)} async-done(((bf16[4,4,64,128]{3,2,1,0:T(8,128)(2,1)}), bf16[4,4,64,128]{3,2,1,0:T(8,128)(2,1)}, u32[]{:S(2)}, u32[]{:S(2)}) %all-to-all-start.1) | async-done | bytes 262176 | tf_op jit(solution)/shard_map/all_to_all | solution.py:16
  75.1 22.6 %all_to_all.100 = bf16[32,64,128]{2,1,0:T(8,128)(2,1)S(1)} all-to-all(bf16[32,64,128]{2,1,0:T(8,128)(2,1)S(1)} %bitcast.219), channel_id=1, replica_groups=mesh['x'=4,'z'=8,'y'=4,'core'=2] {'x','z'}, dimensions={0} | all-to-all | bytes 1048576 | tf_op jit(solution)/shard_map/all_to_all | solution.py:16
  98.7 4.8 %all-to-all-start.3 = ((bf16[32,64,128]{2,1,0:T(8,128)(2,1)}), bf16[32,64,128]{2,1,0:T(8,128)(2,1)S(1)}, u32[]{:S(2)}, u32[]{:S(2)}) async-start(bf16[32,64,128]{2,1,0:T(8,128)(2,1)} %broadcast_in_dim.35), calls=%async_computation.3 | async-start | bytes 1048576 | tf_op jit(solution)/shard_map/all_to_all | solution.py:16
  104.6 16.4 %all-to-all-done.3 = bf16[32,64,128]{2,1,0:T(8,128)(2,1)S(1)} async-done(((bf16[32,64,128]{2,1,0:T(8,128)(2,1)}), bf16[32,64,128]{2,1,0:T(8,128)(2,1)S(1)}, u32[]{:S(2)}, u32[]{:S(2)}) %all-to-all-start.3) | async-done | bytes 524320 | tf_op jit(solution)/shard_map/all_to_all | solution.py:16
  129.8 6.5 %all-to-all-done.4 = bf16[4,256,128]{2,1,0:T(8,128)(2,1)S(1)} async-done(((bf16[4,256,128]{2,1,0:T(8,128)(2,1)}), bf16[4,256,128]{2,1,0:T(8,128)(2,1)S(1)}, u32[]{:S(2)}, u32[]{:S(2)}) %all-to-all-start.4) | async-done | bytes 262176 | tf_op jit(solution)/shard_map/all_to_all | solution.py:16
  140.5 22.8 %all_to_all.101 = bf16[32,64,128]{2,1,0:T(8,128)(2,1)S(1)} all-to-all(bf16[32,64,128]{2,1,0:T(8,128)(2,1)} %bitcast.220), channel_id=1, replica_groups=mesh['x'=4,'z'=8,'y'=4,'core'=2] {'x','z'}, dimensions={0} | all-to-all | bytes 1048576 | tf_op jit(solution)/shard_map/all_to_all | solution.py:16
  163.6 22.2 %all_to_all.102 = bf16[32,64,128]{2,1,0:T(8,128)(2,1)S(1)} all-to-all(bf16[32,64,128]{2,1,0:T(8,128)(2,1)S(1)} %broadcast_in_dim.37), channel_id=1, replica_groups=mesh['x'=4,'z'=8,'y'=4,'core'=2] {'x','z'}, dimensions={0} | all-to-all | bytes 1048576 | tf_op jit(solution)/shard_map/all_to_all | solution.py:16
  194.9 7.1 %all-to-all-done.7 = bf16[4,256,128]{2,1,0:T(8,128)(2,1)S(1)} async-done(((bf16[4,256,128]{2,1,0:T(8,128)(2,1)}), bf16[4,256,128]{2,1,0:T(8,128)(2,1)S(1)}, u32[]{:S(2)}, u32[]{:S(2)}) %all-to-all-start.7) | async-done | bytes 262176 | tf_op jit(solution)/shard_map/all_to_all | solution.py:16
  204.9 22.6 %all_to_all.103 = bf16[32,64,128]{2,1,0:T(8,128)(2,1)S(1)} all-to-all(bf16[32,64,128]{2,1,0:T(8,128)(2,1)S(1)} %bitcast.221), channel_id=1, replica_groups=mesh['x'=4,'z'=8,'y'=4,'core'=2] {'x','z'}, dimensions={0} | all-to-all | bytes 1048576 | tf_op jit(solution)/shard_map/all_to_all | solution.py:16
  227.7 22.1 %all_to_all.104 = bf16[32,64,128]{2,1,0:T(8,128)(2,1)S(1)} all-to-all(bf16[32,64,128]{2,1,0:T(8,128)(2,1)S(1)} %broadcast_in_dim.39), channel_id=1, replica_groups=mesh['x'=4,'z'=8,'y'=4,'core'=2] {'x','z'}, dimensions={0} | all-to-all | bytes 1048576 | tf_op jit(solution)/shard_map/all_to_all | solution.py:16
  251.8 9.7 %all_to_all.105 = bf16[4,256,128]{2,1,0:T(8,128)(2,1)S(1)} all-to-all(bf16[4,256,128]{2,1,0:T(8,128)(2,1)S(1)} %broadcast_in_dim.40), channel_id=1, replica_groups=mesh['x'=4,'z'=8,'y'=4,'core'=2] {'y'}, dimensions={0} | all-to-all | bytes 524288 | tf_op jit(solution)/shard_map/all_to_all | solution.py:16
  266.1 22.7 %all_to_all.106 = bf16[32,64,128]{2,1,0:T(8,128)(2,1)S(1)} all-to-all(bf16[32,64,128]{2,1,0:T(8,128)(2,1)S(1)} %bitcast.222), channel_id=1, replica_groups=mesh['x'=4,'z'=8,'y'=4,'core'=2] {'x','z'}, dimensions={0} | all-to-all | bytes 1048576 | tf_op jit(solution)/shard_map/all_to_all | solution.py:16
  289.1 22.1 %all_to_all.107 = bf16[32,64,128]{2,1,0:T(8,128)(2,1)S(1)} all-to-all(bf16[32,64,128]{2,1,0:T(8,128)(2,1)S(1)} %broadcast_in_dim.41), channel_id=1, replica_groups=mesh['x'=4,'z'=8,'y'=4,'core'=2] {'x','z'}, dimensions={0} | all-to-all | bytes 1048576 | tf_op jit(solution)/shard_map/all_to_all | solution.py:16
  313.0 9.7 %all_to_all.108 = bf16[4,256,128]{2,1,0:T(8,128)(2,1)S(1)} all-to-all(bf16[4,256,128]{2,1,0:T(8,128)(2,1)S(1)} %broadcast_in_dim.42), channel_id=1, replica_groups=mesh['x'=4,'z'=8,'y'=4,'core'=2] {'y'}, dimensions={0} | all-to-all | bytes 524288 | tf_op jit(solution)/shard_map/all_to_all | solution.py:16
  329.0 22.6 %all_to_all.109 = bf16[32,64,128]{2,1,0:T(8,128)(2,1)S(1)} all-to-all(bf16[32,64,128]{2,1,0:T(8,128)(2,1)S(1)} %bitcast.223), channel_id=1, replica_groups=mesh['x'=4,'z'=8,'y'=4,'core'=2] {'x','z'}, dimensions={0} | all-to-all | bytes 1048576 | tf_op jit(solution)/shard_map/all_to_all | solution.py:16
  351.8 22.1 %all_to_all.110 = bf16[32,64,128]{2,1,0:T(8,128)(2,1)S(1)} all-to-all(bf16[32,64,128]{2,1,0:T(8,128)(2,1)S(1)} %broadcast_in_dim.43), channel_id=1, replica_groups=mesh['x'=4,'z'=8,'y'=4,'core'=2] {'x','z'}, dimensions={0} | all-to-all | bytes 1048576 | tf_op jit(solution)/shard_map/all_to_all | solution.py:16
  375.6 9.7 %all_to_all.111 = bf16[4,256,128]{2,1,0:T(8,128)(2,1)S(1)} all-to-all(bf16[4,256,128]{2,1,0:T(8,128)(2,1)S(1)} %broadcast_in_dim.44), channel_id=1, replica_groups=mesh['x'=4,'z'=8,'y'=4,'core'=2] {'y'}, dimensions={0} | all-to-all | bytes 524288 | tf_op jit(solution)/shard_map/all_to_all | solution.py:16
  388.9 22.7 %all_to_all.112 = bf16[32,64,128]{2,1,0:T(8,128)(2,1)} all-to-all(bf16[32,64,128]{2,1,0:T(8,128)(2,1)S(1)} %multiply_reduce_fusion), channel_id=1, replica_groups=mesh['x'=4,'z'=8,'y'=4,'core'=2] {'x','z'}, dimensions={0} | all-to-all | bytes 1048576 | tf_op jit(solution)/shard_map/all_to_all | solution.py:16
  413.2 12.8 %all_to_all.113 = bf16[8,256,128]{1,2,0:T(8,128)(2,1)S(1)} all-to-all(bf16[8,256,128]{1,2,0:T(8,128)(2,1)S(1)} %bitcast.225), channel_id=1, replica_groups=mesh['x'=4,'z'=8,'y'=4,'core'=2] {'y','core'}, dimensions={0} | all-to-all | bytes 1048576 | tf_op jit(solution)/shard_map/all_to_all | solution.py:16
  433.0 8.1 %all-to-all-done.19 = bf16[8,256,128]{1,2,0:T(8,128)(2,1)S(1)} async-done(((bf16[8,256,128]{1,2,0:T(8,128)(2,1)}), bf16[8,256,128]{1,2,0:T(8,128)(2,1)S(1)}, u32[]{:S(2)}, u32[]{:S(2)}) %all-to-all-start.19) | async-done | bytes 524320 | tf_op jit(solution)/shard_map/all_to_all | solution.py:16
  (196 shorter events, 69.3 us)
Async XLA Ops:
  0.6 203.2 %copy-start = (bf16[2048,512]{1,0:T(8,128)(2,1)S(1)}, bf16[2048,512]{1,0:T(8,128)(2,1)}, u32[]{:S(2)}) copy-start(bf16[2048,512]{1,0:T(8,128)(2,1)} %param.21) | copy-start | bytes 6291460
  1.7 27.9 %copy-start.9 = (bf16[1,64,2048]{2,1,0:T(8,128)(2,1)S(1)}, bf16[1,64,2048]{2,1,0:T(8,128)(2,1)}, u32[]{:S(2)}) copy-start(bf16[1,64,2048]{2,1,0:T(8,128)(2,1)} %param.22) | copy-start | bytes 786436
  30.8 29.3 %all-to-all-start = ((bf16[32,64,128]{2,1,0:T(8,128)(2,1)}), bf16[32,64,128]{2,1,0:T(8,128)(2,1)S(1)}, u32[]{:S(2)}, u32[]{:S(2)}) async-start(bf16[32,64,128]{2,1,0:T(8,128)(2,1)} %broadcast_in_dim.33), calls=%async_computation | async-start | bytes 1048576 | tf_op jit(solution)/shard_map/all_to_all | solution.py:16
  61.3 10.8 %all-to-all-start.1 = ((bf16[4,4,64,128]{3,2,1,0:T(8,128)(2,1)}), bf16[4,4,64,128]{3,2,1,0:T(8,128)(2,1)}, u32[]{:S(2)}, u32[]{:S(2)}) async-start(bf16[4,4,64,128]{3,2,1,0:T(8,128)(2,1)} %broadcast_in_dim.34), calls=%async_computation.1 | async-start | bytes 524288 | tf_op jit(solution)/shard_map/all_to_all | solution.py:16
  73.0 1.3 collective-permute-start
  74.8 28.8 %copy-start.22 = (bf16[8,64,128]{2,1,0:T(8,128)(2,1)S(1)}, bf16[8,64,128]{2,1,0:T(8,128)(2,1)}, u32[]{:S(2)}) copy-start(bf16[8,64,128]{2,1,0:T(8,128)(2,1)} %get-tuple-element.25) | copy-start | bytes 393220
  98.7 22.3 %all-to-all-start.3 = ((bf16[32,64,128]{2,1,0:T(8,128)(2,1)}), bf16[32,64,128]{2,1,0:T(8,128)(2,1)S(1)}, u32[]{:S(2)}, u32[]{:S(2)}) async-start(bf16[32,64,128]{2,1,0:T(8,128)(2,1)} %broadcast_in_dim.35), calls=%async_computation.3 | async-start | bytes 1048576 | tf_op jit(solution)/shard_map/all_to_all | solution.py:16
  104.5 18.3 %collective-permute-start.1 = (bf16[2,4,64,128]{3,2,1,0:T(8,128)(2,1)S(1)}, bf16[2,4,64,128]{3,2,1,0:T(8,128)(2,1)S(1)}, u32[]{:S(2)}, u32[]{:S(2)}) collective-permute-start(bf16[2,4,64,128]{3,2,1,0:T(8,128)(2,1)S(1)} %slice.133), channel_id=1, source_target_pairs={{0,1},{1,0},{2,3},{3,2},{4,5},{5,4},{6,7},{7,6},{8,9},{9,8},{10,11... | collective-permute-start | bytes 393224 | tf_op jit(solution)/shard_map/ppermute | solution.py:39
  122.8 1.7 collective-permute-start.2
  125.3 11.0 %all-to-all-start.4 = ((bf16[4,256,128]{2,1,0:T(8,128)(2,1)}), bf16[4,256,128]{2,1,0:T(8,128)(2,1)S(1)}, u32[]{:S(2)}, u32[]{:S(2)}) async-start(bf16[4,256,128]{2,1,0:T(8,128)(2,1)} %broadcast_in_dim.36), calls=%async_computation.4 | async-start | bytes 524288 | tf_op jit(solution)/shard_map/all_to_all | solution.py:16
  136.5 1.3 collective-permute-start.3
  189.1 1.3 collective-permute-start.4
  191.3 10.6 %all-to-all-start.7 = ((bf16[4,256,128]{2,1,0:T(8,128)(2,1)}), bf16[4,256,128]{2,1,0:T(8,128)(2,1)S(1)}, u32[]{:S(2)}, u32[]{:S(2)}) async-start(bf16[4,256,128]{2,1,0:T(8,128)(2,1)} %broadcast_in_dim.38), calls=%async_computation.7 | async-start | bytes 524288 | tf_op jit(solution)/shard_map/all_to_all | solution.py:16
  202.1 1.5 collective-permute-start.5
  250.3 1.3 collective-permute-start.6
  261.6 1.3 collective-permute-start.7
  266.1 45.0 %copy-start.6 = (bf16[2,1024,256]{2,1,0:T(8,128)(2,1)S(1)}, bf16[2,1024,256]{2,1,0:T(8,128)(2,1)}, u32[]{:S(2)}) copy-start(bf16[2,1024,256]{2,1,0:T(8,128)(2,1)} %param.20) | copy-start | bytes 3145732
  311.5 1.3 collective-permute-start.8
  324.3 1.3 collective-permute-start.9
  327.6 46.3 %copy-start.8 = (bf16[4,512,128]{2,1,0:T(8,128)(2,1)S(1)}, bf16[4,512,128]{2,1,0:T(8,128)(2,1)}, u32[]{:S(2)}) copy-start(bf16[4,512,128]{2,1,0:T(8,128)(2,1)} %param.19) | copy-start | bytes 1572868
  374.2 1.3 collective-permute-start.10
  385.3 27.5 %copy-start.10 = (bf16[1,64,2048]{2,1,0:T(8,128)(2,1)S(1)}, bf16[1,64,2048]{2,1,0:T(8,128)(2,1)}, u32[]{:S(2)}) copy-start(bf16[1,64,2048]{2,1,0:T(8,128)(2,1)} %param.22) | copy-start | bytes 786436
  385.5 1.3 collective-permute-start.11
  427.3 13.8 %all-to-all-start.19 = ((bf16[8,256,128]{1,2,0:T(8,128)(2,1)}), bf16[8,256,128]{1,2,0:T(8,128)(2,1)S(1)}, u32[]{:S(2)}, u32[]{:S(2)}) async-start(bf16[8,256,128]{1,2,0:T(8,128)(2,1)} %bitcast.209), calls=%async_computation.19 | async-start | bytes 1048576 | tf_op jit(solution)/shard_map/all_to_all | solution.py:16
  (21 other events, 227.5 us)
